TPU v7x, 32 devices: a whole 2x2x4 slice. The times are simulated.
32 devices in a mesh: patch: 8 (over z, y), sample: 4 (over x, core).
Axes of the slice: x: 2, y: 2, z: 4, core: 2. Of those that a mesh axis runs over, the one named last changes fastest.
Arguments:
- features: bfloat16 [4, 4096, 512], P('sample', 'patch'), may hold values from -600 to 600
- cotangent: bfloat16 [4, 4096, 512], P('sample', 'patch'), may hold values from -6 to 6
- weight_qkv: bfloat16 [512, 1536], replicated, may hold values from -5 to 5
- weight_out: bfloat16 [512, 512], replicated, may hold values from -0.25 to 0.25
- key_tiles: int32 [32, 8], replicated, may hold values from 0 to 31, as said below
- tile_valid: int32 [32, 8], replicated, may hold values from 0 to 1, as said below
Outputs:
- grad_features: bfloat16 [4, 4096, 512], P('sample', 'patch')
- grad_qkv: float32 [512, 1536], replicated
- grad_out: float32 [512, 512], replicated
Inputs may be any that keep to these rules, and one draw needn't show every extreme that they name: `key_tiles`: row g names 8 distinct tile ids. A tile's patch is its id // 4. The first id is g itself, the next 3 are other tiles of g's patch, and the last 4 lie one each in the patches at offsets -2 to 2 other than 0 around the cycle of patches, in rising order of offset. Over the rows of one patch exactly 2 distinct tiles of each such neighbouring patch are named. `tile_valid`: column 0 is always 1.
All inputs are finite; a program needn't handle non-finite values.
Results may differ from a plain program's by a relative error of at most 0.0088.
Values may be sent and summed in bfloat16 or wider, within the bound.
No kernel may reach another device: no remote copies, remote signals or barrier semaphores. Data moves between devices by JAX's collectives and lax.ppermute only.
A program may use at most 192 MiB of HBM per device.

v0:
```python
from functools import partial
import math
import jax
import jax.numpy as jnp
from jax import lax
from jax.sharding import PartitionSpec as P

HEADS = 4
TILE = 128
NB = 8
REACH = 2
CAP = 2
epsilon = 1e-06


def from_behind(value, axis, steps):
    count = lax.axis_size(axis)
    pairs = [(source, (source + steps) % count) for source in range(count)]
    return lax.ppermute(value, axis, pairs)


def tile_backward(query_tile, pair_tiles, live_flags, grad_tile, head_count):
    row_count = query_tile.shape[0]
    model_width = query_tile.shape[1]
    head_width = model_width // head_count
    scaling = head_width ** (-0.5)
    key_heads = pair_tiles[:, :, :model_width].reshape(-1, head_count, head_width)
    value_heads = pair_tiles[:, :, model_width:].reshape(-1, head_count, head_width)
    query_heads = query_tile.reshape(row_count, head_count, head_width)
    grad_heads = grad_tile.reshape(row_count, head_count, head_width)
    scores = (
        jnp.einsum("qhd,khd->hqk", query_heads, key_heads, preferred_element_type=jnp.float32)
        * scaling
    )
    live_mask = jnp.repeat(live_flags > 0, pair_tiles.shape[1])
    scores = jnp.where(live_mask[None, None, :], scores, -jnp.inf)
    highest = jnp.max(scores, -1, keepdims=True)
    expanded = jnp.exp(scores - highest)
    attention = expanded / jnp.sum(expanded, -1, keepdims=True)
    attention_low = attention.astype(jnp.bfloat16)
    attended = jnp.einsum(
        "hqk,khd->qhd", attention_low, value_heads, preferred_element_type=jnp.float32
    )
    attended = attended.astype(jnp.bfloat16).reshape(row_count, model_width)
    dprob = jnp.einsum("qhd,khd->hqk", grad_heads, value_heads, preferred_element_type=jnp.float32)
    centre = jnp.sum(attention * dprob, -1, keepdims=True)
    dscore = (attention * (dprob - centre) * scaling).astype(jnp.bfloat16)
    dquery = jnp.einsum(
        "hqk,khd->qhd", dscore, key_heads, preferred_element_type=jnp.float32
    ).reshape(row_count, model_width)
    dkey = jnp.einsum("hqk,qhd->khd", dscore, query_heads, preferred_element_type=jnp.float32)
    dvalue = jnp.einsum(
        "hqk,qhd->khd", attention_low, grad_heads, preferred_element_type=jnp.float32
    )
    dkey = dkey.reshape(pair_tiles.shape[0], pair_tiles.shape[1], model_width)
    dvalue = dvalue.reshape(pair_tiles.shape[0], pair_tiles.shape[1], model_width)
    return (attended, dquery, jnp.concatenate([dkey, dvalue], -1))


def tile_flags(list_rows, source, tile_count):
    first_id = source * tile_count
    wanted = (
        list_rows[:, :, None] == first_id + jnp.arange(tile_count, dtype=jnp.int32)[None, None, :]
    )
    wanted_flags = jnp.any(wanted, axis=(0, 1))
    wanted_places = jnp.cumsum(wanted_flags.astype(jnp.int32)) - 1
    return (wanted_flags, wanted_places)


def on_device(features, cotangent, weight_qkv, weight_out, key_tiles, tile_valid):
    patches = lax.axis_size("patch")
    position = lax.axis_index("patch")
    rows_local = features.shape[1]
    model_width = features.shape[2]
    tile_count = rows_local // TILE
    offsets = [shift_by for shift_by in range(-REACH, REACH + 1) if shift_by != 0]
    inputs = features[0].astype(jnp.float32)
    inverse = lax.rsqrt(jnp.mean(inputs * inputs, -1, keepdims=True) + epsilon)
    normed = inputs * inverse
    normed_low = normed.astype(jnp.bfloat16)
    projected = jnp.dot(normed_low, weight_qkv, preferred_element_type=jnp.float32).astype(
        jnp.bfloat16
    )
    queries = projected[:, :model_width]
    pairs_own = projected[:, model_width:].reshape(tile_count, TILE, 2 * model_width)
    grad_rows = cotangent[0]
    grad_attended = jnp.einsum(
        "pe,de->pd", grad_rows, weight_out, preferred_element_type=jnp.float32
    ).astype(jnp.bfloat16)
    my_lists = lax.dynamic_slice_in_dim(key_tiles, position * tile_count, tile_count, 0)
    my_valid = lax.dynamic_slice_in_dim(tile_valid, position * tile_count, tile_count, 0)
    owner_patch = my_lists // tile_count
    within = my_lists % tile_count
    distance = (owner_patch - position) % patches
    distance = jnp.where(distance > patches // 2, distance - patches, distance)
    order_index = jnp.where(distance < 0, distance + REACH, distance + REACH - 1)
    senders = []
    tile_range = jnp.arange(tile_count, dtype=jnp.int32)
    arrivals = []
    place_rows = []
    for shift_by in offsets:
        target = (position - shift_by) % patches
        target_lists = lax.dynamic_slice_in_dim(key_tiles, target * tile_count, tile_count, 0)
        wanted_flags, wanted_places = tile_flags(target_lists, position, tile_count)
        picker = wanted_flags[None, :] & (
            wanted_places[None, :] == jnp.arange(CAP, dtype=jnp.int32)[:, None]
        )
        send_rows = jnp.sum(jnp.where(picker, tile_range[None, :], 0), 1)
        senders.append(send_rows)
        packed = jnp.take(pairs_own, send_rows, axis=0)
        arrived = from_behind(packed, "patch", -shift_by)
        arrivals.append(arrived)
        source = (position + shift_by) % patches
        incoming_flags, incoming_places = tile_flags(my_lists, source, tile_count)
        place_rows.append(incoming_places)
    buffer = jnp.concatenate([pairs_own] + arrivals, 0)
    place_table = jnp.concatenate(place_rows, 0)
    lookup = order_index * tile_count + within
    matched = lookup[:, :, None] == jnp.arange(place_table.shape[0], dtype=jnp.int32)[None, None, :]
    remote_place = jnp.sum(jnp.where(matched, place_table[None, None, :], 0), -1)
    slot_ids = jnp.where(distance == 0, within, tile_count + order_index * CAP + remote_place)
    group_size = math.gcd(4, tile_count)
    step_count = tile_count // group_size
    tile_pass = jax.vmap(partial(tile_backward, head_count=HEADS))
    buffer_count = buffer.shape[0]

    def advance(running, pieces):
        query_group, slot_group, live_group, grad_group = pieces
        flat_slots = slot_group.reshape(-1)
        gathered = jnp.take(buffer, flat_slots, axis=0).reshape(
            group_size, NB, TILE, 2 * model_width
        )
        attended, dquery, dpairs = tile_pass(query_group, gathered, live_group, grad_group)
        running = running.at[flat_slots].add(dpairs.reshape(group_size * NB, TILE, 2 * model_width))
        return (running, (attended, dquery))

    start_sums = jnp.zeros((buffer_count, TILE, 2 * model_width), jnp.float32)
    scanned = (
        queries.reshape(step_count, group_size, TILE, model_width),
        slot_ids.reshape(step_count, group_size, NB),
        my_valid.reshape(step_count, group_size, NB),
        grad_attended.reshape(step_count, group_size, TILE, model_width),
    )
    totals, (attended_all, dquery_all) = lax.scan(advance, start_sums, scanned)
    grads_own = totals[:tile_count]
    for offset_index, shift_by in enumerate(offsets):
        portion = totals[tile_count + offset_index * CAP : tile_count + (offset_index + 1) * CAP]
        returned = from_behind(portion.astype(jnp.bfloat16), "patch", shift_by).astype(
            portion.dtype
        )
        grads_own = grads_own.at[senders[offset_index]].add(returned)
    attended_rows = attended_all.reshape(rows_local, model_width)
    grad_projected = jnp.concatenate(
        [
            dquery_all.reshape(rows_local, model_width),
            grads_own.reshape(rows_local, 2 * model_width),
        ],
        1,
    ).astype(jnp.bfloat16)
    grad_normed = jnp.einsum(
        "pe,de->pd", grad_projected, weight_qkv, preferred_element_type=jnp.float32
    )
    grad_inputs = grad_rows.astype(jnp.float32) + inverse * (
        grad_normed - normed * jnp.mean(grad_normed * normed, -1, keepdims=True)
    )
    local_qkv = jnp.einsum(
        "pd,pe->de", normed_low, grad_projected, preferred_element_type=jnp.float32
    )
    local_out = jnp.einsum(
        "pd,pe->de", attended_rows, grad_rows, preferred_element_type=jnp.float32
    )
    summed_qkv, summed_out = lax.psum((local_qkv, local_out), ("patch", "sample"))
    factor = float(lax.axis_size("patch") * lax.axis_size("sample") * rows_local) ** (-0.5)
    return (grad_inputs.astype(jnp.bfloat16)[None], summed_qkv * factor, summed_out * factor)


def solution(mesh):
    placed = (P("sample", "patch", None), P("sample", "patch", None), P(), P(), P(), P())
    return jax.shard_map(
        on_device,
        mesh=mesh,
        in_specs=placed,
        out_specs=(P("sample", "patch", None), P(), P()),
        check_vma=False,
    )
```

profile of v0, /device:TPU:0, one launch (start us, length us, event | category | flops | bytes accessed | tf_op | source)
XLA Modules:
  0.0 484.2 jit_solution(8484835399230841525)
XLA Ops:
  14.5 1.9 broadcast_select_fusion.1
  16.4 5.1 %collective-permute-start.3 = (bf16[2,128,1024]{2,1,0:T(8,128)(2,1)}, bf16[2,128,1024]{2,1,0:T(8,128)(2,1)}, u32[]{:S(2)}, u32[]{:S(2)}) collective-permute-start(bf16[2,128,1024]{2,1,0:T(8,128)(2,1)} %broadcast_select_fusion.1), channel_id=1, source_target_pairs={{0,24},{4,28},{8,0},{12,4},{16,8},{20,12},{24,16},{28,20},{1,25},{... | collective-permute-start | bytes 1572872 | tf_op jit(solution)/shard_map/ppermute | solution.py:19
  22.9 2.0 broadcast_select_fusion.2
  28.2 2.0 broadcast_select_fusion.3
  32.2 1.9 broadcast_select_fusion.4
  36.9 2.5 convolution_convert_fusion.1
  41.3 2.0 reshape.469
  43.3 2.1 copy.88
  45.4 2.0 reshape.470
  47.3 2.0 copy.90
  50.4 6.0 %collective-permute-done = bf16[2,128,1024]{2,1,0:T(8,128)(2,1)} collective-permute-done((bf16[2,128,1024]{2,1,0:T(8,128)(2,1)}, bf16[2,128,1024]{2,1,0:T(8,128)(2,1)}, u32[]{:S(2)}, u32[]{:S(2)}) %collective-permute-start) | collective-permute-done | bytes 524320 | tf_op jit(solution)/shard_map/ppermute | solution.py:19
  63.9 7.0 %gather_fusion = bf16[32,128,1024]{2,1,0:T(8,128)(2,1)} fusion(bf16[12,128,1024]{2,1,0:T(8,128)(2,1)} %constant_dynamic-update-slice_fusion, s32[1024]{0:T(1024)S(1)} %pad_clamp_fusion), kind=kCustom, calls=%fused_computation.4 | custom fusion | bytes 16777344 | tf_op jit(solution)/shard_map/while/body/eval_jaxpr/jit(_take)/gather | solution.py:130
  70.9 7.5 %broadcast_select_fusion = bf16[4,8,128,1024]{3,2,1,0:T(8,128)(2,1)} fusion(bf16[4,8,128,1024]{3,2,1,0:T(8,128)(2,1)} %bitcast.111, pred[4,8]{1,0:T(4,128)(4,1)S(1)} %get-tuple-element.53), kind=kLoop, calls=%fused_computation.18 | loop fusion | flops 4194304 | bytes 16777248 | tf_op jit(solution)/shard_map/while/body/eval_jaxpr/jit(_take)/select_n | solution.py:130
  78.4 5.9 %fusion.74 = (bf16[4,8,128,512]{3,2,1,0:T(8,128)(2,1)}, bf16[4,8,128,512]{3,2,1,0:T(8,128)(2,1)}) fusion(bf16[4,8,128,1024]{3,2,1,0:T(8,128)(2,1)} %broadcast_select_fusion), kind=kLoop, calls=%fused_computation.171 | loop fusion | bytes 16777216 | tf_op jit(solution)/shard_map/while/body/eval_jaxpr/vmap()/slice | solution.py:28
  84.2 6.9 %reshape.576 = bf16[4,1024,4,128]{3,2,1,0:T(4,128)(2,1)} reshape(bf16[4,8,128,512]{3,2,1,0:T(8,128)(2,1)} %get-tuple-element.56) | data formatting | bytes 8388608 | tf_op jit(solution)/shard_map/while/body/eval_jaxpr/vmap()/reshape | solution.py:27
  91.2 7.5 %copy.96 = bf16[4,1024,4,128]{1,3,2,0:T(8,128)(2,1)} copy(bf16[4,1024,4,128]{3,2,1,0:T(4,128)(2,1)} %reshape.576) | data formatting | bytes 8388608 | tf_op jit(solution)/shard_map/while/body/eval_jaxpr/vmap()/reshape | solution.py:27
  98.7 6.9 %reshape.577 = bf16[4,1024,4,128]{3,2,1,0:T(4,128)(2,1)} reshape(bf16[4,8,128,512]{3,2,1,0:T(8,128)(2,1)} %get-tuple-element.55) | data formatting | bytes 8388608 | tf_op jit(solution)/shard_map/while/body/eval_jaxpr/vmap()/reshape | solution.py:28
  105.6 7.6 %copy.95 = bf16[4,1024,4,128]{1,3,2,0:T(8,128)(2,1)} copy(bf16[4,1024,4,128]{3,2,1,0:T(4,128)(2,1)} %reshape.577) | data formatting | bytes 8388608 | tf_op jit(solution)/shard_map/while/body/eval_jaxpr/vmap()/reshape | solution.py:28
  113.2 6.8 %fusion.77 = f32[4,4,128,1024]{3,2,1,0:T(8,128)} fusion(bf16[4,128,4,128]{1,3,2,0:T(8,128)(2,1)S(1)} %copy-done.3, bf16[4,1024,4,128]{1,3,2,0:T(8,128)(2,1)} %copy.95), kind=kOutput, calls=%fused_computation.174 | convolution fusion | flops 536870912 | bytes 13107200 | tf_op jit(solution)/shard_map/while/body/eval_jaxpr/vmap(qhd,khd->hqk)/dot_general | solution.py:45
  120.0 8.5 %fusion.76 = (f32[4,4,128]{2,1,0:T(4,128)S(1)}, f32[4,4,128,1024]{3,2,1,0:T(8,128)}) fusion(pred[4,1024]{1,0:T(4,128)(4,1)S(1)} %bitcast.123, bf16[4,128,4,128]{1,3,2,0:T(8,128)(2,1)S(1)} %copy-done.7, bf16[4,1024,4,128]{1,3,2,0:T(8,128)(2,1)} %copy.96), kind=kOutput, calls=%fused_computation.173 | convolution fusion | flops 545260544 | bytes 13119488 | tf_op jit(solution)/shard_map/while/body/eval_jaxpr/vmap()/sub | solution.py:38
  128.5 6.9 %fusion.30 = bf16[4,128,4,128]{1,3,2,0:T(8,128)(2,1)} fusion(bf16[4,1024,4,128]{1,3,2,0:T(8,128)(2,1)} %copy.95, f32[4,4,128,1024]{3,2,1,0:T(8,128)} %get-tuple-element.67, f32[4,4,128]{2,1,0:T(4,128)S(1)} %get-tuple-element.66), kind=kOutput, calls=%fused_computation.42 | convolution fusion | flops 541327360 | bytes 13115392 | tf_op jit(solution)/shard_map/while/body/eval_jaxpr/vmap(hqk,khd->qhd)/dot_general | solution.py:41
  135.5 4.0 convolution_bitcast_fusion
  139.6 23.7 %fusion.15 = f32[4,1024,4,128]{1,3,2,0:T(8,128)} fusion(bf16[4,128,4,128]{1,3,2,0:T(8,128)(2,1)S(1)} %copy-done.7, f32[4,4,128,1024]{3,2,1,0:T(8,128)} %fusion.77, f32[4,4,128,1024]{3,2,1,0:T(8,128)} %get-tuple-element.67, f32[4,4,128]{2,1,0:T(4,128)S(1)} %get-tuple-element.66), kind=kOutput, calls=%fused_computation.26 | convolution fusion | flops 551554048 | bytes 25698304 | tf_op jit(solution)/shard_map/while/body/eval_jaxpr/vmap(hqk,qhd->khd)/dot_general | solution.py:51
  163.3 9.9 %copy.89 = f32[4,1024,4,128]{3,2,1,0:T(4,128)} copy(f32[4,1024,4,128]{1,3,2,0:T(8,128)} %fusion.15) | data formatting | bytes 16777216 | tf_op jit(solution)/shard_map/while/body/eval_jaxpr/vmap(hqk,qhd->khd)/transpose | solution.py:51
  173.2 10.3 %concatenate.21 = f32[32,128,512]{2,1,0:T(8,128)} reshape(f32[4,1024,4,128]{3,2,1,0:T(4,128)} %copy.89) | data formatting | bytes 16777216 | tf_op jit(solution)/shard_map/while/body/eval_jaxpr/vmap()/concatenate | solution.py:57
  183.4 9.9 %copy.91 = f32[4,1024,4,128]{3,2,1,0:T(4,128)} copy(f32[4,1024,4,128]{1,3,2,0:T(8,128)} %convolution_bitcast_fusion) | data formatting | bytes 16777216 | tf_op jit(solution)/shard_map/while/body/eval_jaxpr/vmap(hqk,qhd->khd)/transpose | solution.py:52
  193.3 10.3 %concatenate.22 = f32[32,128,512]{2,1,0:T(8,128)} reshape(f32[4,1024,4,128]{3,2,1,0:T(4,128)} %copy.91) | data formatting | bytes 16777216 | tf_op jit(solution)/shard_map/while/body/eval_jaxpr/vmap()/concatenate | solution.py:57
  203.6 11.7 %pad_maximum_fusion = f32[32,128,1024]{2,1,0:T(8,128)} fusion(f32[32,128,512]{2,1,0:T(8,128)} %concatenate.22, f32[32,128,512]{2,1,0:T(8,128)} %concatenate.21), kind=kLoop, calls=%fused_computation.12 | loop fusion | flops 4194304 | bytes 33554432 | tf_op jit(solution)/shard_map/while/body/eval_jaxpr/vmap()/concatenate | solution.py:57
  215.3 3.4 broadcast_in_dim.161
  218.7 35.9 %scatter_fusion = f32[12,128,1024]{2,1,0:T(8,128)} fusion(f32[12,128,1024]{2,1,0:T(8,128)} %broadcast_in_dim.161, s32[32]{0:T(128)S(1)} %fusion.61, f32[32,128,1024]{2,1,0:T(8,128)} %pad_maximum_fusion), kind=kCustom, calls=%fused_computation.5 | custom fusion | flops 4194304 | bytes 50331776 | tf_op jit(solution)/shard_map/while/body/eval_jaxpr/scatter-add | solution.py:134
  254.6 4.9 %convert.25 = bf16[12,128,1024]{2,1,0:T(8,128)(2,1)} convert(f32[12,128,1024]{2,1,0:T(8,128)} %scatter_fusion) | non-fusion elementwise | flops 1572864 | bytes 9437184 | tf_op jit(solution)/shard_map/convert.17
  259.6 3.2 slice.56
  263.9 2.9 fusion.75
  266.8 3.3 collective-permute-start.4
  273.1 22.8 %fusion.33 = bf16[4,128,4,128]{1,3,2,0:T(8,128)(2,1)S(1)} fusion(bf16[4,1024,4,128]{1,3,2,0:T(8,128)(2,1)} %copy.96, f32[4,4,128,1024]{3,2,1,0:T(8,128)} %fusion.77, f32[4,4,128,1024]{3,2,1,0:T(8,128)} %get-tuple-element.67, f32[4,4,128]{2,1,0:T(4,128)S(1)} %get-tuple-element.66), kind=kOutput, calls=%fused_computation.43 | convolution fusion | flops 551816192 | bytes 21504000 | tf_op jit(solution)/shard_map/while/body/eval_jaxpr/vmap(hqk,khd->qhd)/dot_general | solution.py:48
  298.2 2.5 fusion.45
  300.7 2.1 convert_element_type.189
  302.8 3.4 scatter_fusion.1
  306.2 2.1 convert_element_type.190
  308.3 3.4 scatter_fusion.2
  311.8 2.1 convert_element_type.191
  313.9 3.4 scatter_fusion.3
  317.3 2.1 convert_element_type.192
  319.4 3.4 scatter_fusion.4
  325.5 2.7 fusion.42
  329.2 2.3 fusion.36
  332.9 139.6 %all-reduce.3.cloned.1.call-done = (f32[512,1536]{1,0:T(8,128)}, f32[512,512]{1,0:T(8,128)}) async-done(((f32[512,1536]{1,0:T(8,128)}, f32[512,512]{1,0:T(8,128)}), (f32[512,1536]{1,0:T(8,128)}, f32[512,512]{1,0:T(8,128)})) %all-reduce.3.cloned.1.call-update) | async-done | bytes 4194320 | tf_op jit(solution)/shard_map/psum | solution.py:172
  472.4 3.9 broadcast_multiply_fusion
  (126 shorter events, 39.5 us)
Async XLA Ops:
  7.2 3.7 copy-start
  7.2 465.2 %all-reduce.3.cloned.1.call-start = ((), (), s32[]{:S(2)}) async-start(), calls=%async_computation | async-start | bytes 8388608 | tf_op jit(solution)/shard_map/psum | solution.py:172
  11.9 1.1 copy-start.5
  13.1 23.5 %copy-start.9 = (s32[32,8]{0,1:T(8,128)S(1)}, s32[32,8]{0,1:T(8,128)}, u32[]{:S(2)}) copy-start(s32[32,8]{0,1:T(8,128)} %param.13) | copy-start | bytes 3076
  16.4 45.6 %collective-permute-start.3 = (bf16[2,128,1024]{2,1,0:T(8,128)(2,1)}, bf16[2,128,1024]{2,1,0:T(8,128)(2,1)}, u32[]{:S(2)}, u32[]{:S(2)}) collective-permute-start(bf16[2,128,1024]{2,1,0:T(8,128)(2,1)} %broadcast_select_fusion.1), channel_id=1, source_target_pairs={{0,24},{4,28},{8,0},{12,4},{16,8},{20,12},{24,16},{28,20},{1,25},{... | collective-permute-start | bytes 1572872 | tf_op jit(solution)/shard_map/ppermute | solution.py:19
  24.9 35.3 %collective-permute-start.2 = (bf16[2,128,1024]{2,1,0:T(8,128)(2,1)}, bf16[2,128,1024]{2,1,0:T(8,128)(2,1)}, u32[]{:S(2)}, u32[]{:S(2)}) collective-permute-start(bf16[2,128,1024]{2,1,0:T(8,128)(2,1)} %broadcast_select_fusion.2), channel_id=1, source_target_pairs={{0,28},{4,0},{8,4},{12,8},{16,12},{20,16},{24,20},{28,24},{1,29},{... | collective-permute-start | bytes 1572872 | tf_op jit(solution)/shard_map/ppermute | solution.py:19
  30.2 28.1 %collective-permute-start.1 = (bf16[2,128,1024]{2,1,0:T(8,128)(2,1)}, bf16[2,128,1024]{2,1,0:T(8,128)(2,1)}, u32[]{:S(2)}, u32[]{:S(2)}) collective-permute-start(bf16[2,128,1024]{2,1,0:T(8,128)(2,1)} %broadcast_select_fusion.3), channel_id=1, source_target_pairs={{0,4},{4,8},{8,12},{12,16},{16,20},{20,24},{24,28},{28,0},{1,5},{5... | collective-permute-start | bytes 1572872 | tf_op jit(solution)/shard_map/ppermute | solution.py:19
  34.2 22.3 %collective-permute-start = (bf16[2,128,1024]{2,1,0:T(8,128)(2,1)}, bf16[2,128,1024]{2,1,0:T(8,128)(2,1)}, u32[]{:S(2)}, u32[]{:S(2)}) collective-permute-start(bf16[2,128,1024]{2,1,0:T(8,128)(2,1)} %broadcast_select_fusion.4), channel_id=1, source_target_pairs={{0,8},{4,12},{8,16},{12,20},{16,24},{20,28},{24,0},{28,4},{1,9},{5... | collective-permute-start | bytes 1572872 | tf_op jit(solution)/shard_map/ppermute | solution.py:19
  105.6 7.6 %copy-start.3 = (bf16[4,128,4,128]{1,3,2,0:T(8,128)(2,1)S(1)}, bf16[4,128,4,128]{1,3,2,0:T(8,128)(2,1)}, u32[]{:S(2)}) copy-start(bf16[4,128,4,128]{1,3,2,0:T(8,128)(2,1)} %copy.90) | copy-start | bytes 1572868
  113.2 6.8 %copy-start.7 = (bf16[4,128,4,128]{1,3,2,0:T(8,128)(2,1)S(1)}, bf16[4,128,4,128]{1,3,2,0:T(8,128)(2,1)}, u32[]{:S(2)}) copy-start(bf16[4,128,4,128]{1,3,2,0:T(8,128)(2,1)} %copy.88) | copy-start | bytes 1572868
  128.5 7.0 %copy-start.10 = (f32[4,4,128,1024]{3,2,1,0:T(8,128)S(1)}, f32[4,4,128,1024]{3,2,1,0:T(8,128)}, u32[]{:S(2)}) copy-start(f32[4,4,128,1024]{3,2,1,0:T(8,128)} %get-tuple-element.67) | copy-start | bytes 25165828
  259.6 3.2 copy-start.8
  266.8 33.9 %collective-permute-start.4 = (bf16[2,128,1024]{2,1,0:T(8,128)(2,1)}, bf16[2,128,1024]{2,1,0:T(8,128)(2,1)}, u32[]{:S(2)}, u32[]{:S(2)}) collective-permute-start(bf16[2,128,1024]{2,1,0:T(8,128)(2,1)} %get-tuple-element.60), channel_id=1, source_target_pairs={{0,24},{4,28},{8,0},{12,4},{16,8},{20,12},{24,16},{28,20},{1,25},{... | collective-permute-start | bytes 1572872 | tf_op jit(solution)/shard_map/ppermute | solution.py:19
  270.1 36.1 %collective-permute-start.5 = (bf16[2,128,1024]{2,1,0:T(8,128)(2,1)}, bf16[2,128,1024]{2,1,0:T(8,128)(2,1)}, u32[]{:S(2)}, u32[]{:S(2)}) collective-permute-start(bf16[2,128,1024]{2,1,0:T(8,128)(2,1)} %get-tuple-element.59), channel_id=1, source_target_pairs={{0,28},{4,0},{8,4},{12,8},{16,12},{20,16},{24,20},{28,24},{1,29},{... | collective-permute-start | bytes 1572872 | tf_op jit(solution)/shard_map/ppermute | solution.py:19
  271.6 40.1 %collective-permute-start.6 = (bf16[2,128,1024]{2,1,0:T(8,128)(2,1)}, bf16[2,128,1024]{2,1,0:T(8,128)(2,1)}, u32[]{:S(2)}, u32[]{:S(2)}) collective-permute-start(bf16[2,128,1024]{2,1,0:T(8,128)(2,1)} %get-tuple-element.58), channel_id=1, source_target_pairs={{0,4},{4,8},{8,12},{12,16},{16,20},{20,24},{24,28},{28,0},{1,5},{5... | collective-permute-start | bytes 1572872 | tf_op jit(solution)/shard_map/ppermute | solution.py:19
  272.1 26.1 %copy-start.1 = (bf16[1,512,512]{2,1,0:T(8,128)(2,1)S(1)}, bf16[1,512,512]{2,1,0:T(8,128)(2,1)}, u32[]{:S(2)}) copy-start(bf16[1,512,512]{2,1,0:T(8,128)(2,1)} %param.9) | copy-start | bytes 1572868
  272.1 45.2 %collective-permute-start.7 = (bf16[2,128,1024]{2,1,0:T(8,128)(2,1)}, bf16[2,128,1024]{2,1,0:T(8,128)(2,1)}, u32[]{:S(2)}, u32[]{:S(2)}) collective-permute-start(bf16[2,128,1024]{2,1,0:T(8,128)(2,1)} %get-tuple-element.57), channel_id=1, source_target_pairs={{0,8},{4,12},{8,16},{12,20},{16,24},{20,28},{24,0},{28,4},{1,9},{5... | collective-permute-start | bytes 1572872 | tf_op jit(solution)/shard_map/ppermute | solution.py:19
  324.6 1.0 copy-start.2
  329.2 2.3 copy-start.4
  472.4 3.9 copy-start.6
Sparse Core Ops, SparseCore 0:
  328.3 144.0 all-reduce.2
where the time goes:
time: 487 us; the launch traced here: 484 us
  waiting for transfers between devices  146 us (30%)
  local copies, waits for them, and re-layouts  126 us (26%)
  other arithmetic  99.9 us (21%)
  matrix products  83.7 us (17%)
  starting transfers between devices  14.5 us (3%)
  between operations  14.4 us (3%)
    psum x1, waiting for transfers between devices, on_device(): lax.psum((local_qkv, local_out), ('patch', 'sample'))  140 us
    scatter-add x1, other arithmetic, advance(): running.at[flat_slots]  35.9 us
    dot_general x1, matrix products, tile_backward(): jnp.einsum('hqk,qhd->khd', dscore, query_heads, preferred_element_type=jn...  23.7 us
    dot_general x1, matrix products, tile_backward(): jnp.einsum('hqk,khd->qhd', dscore, key_heads, preferred_element_type=jnp....  22.8 us
    concatenate x2, local copies, waits for them, and re-layouts, tile_backward(): return (attended, dquery, jnp.concatenate([dkey, dvalue], -1))  20.5 us
    reshape x2, local copies, waits for them, and re-layouts, tile_backward(): pair_tiles[:, :, model_width:].reshape(-1, head_count, head_width)  14.5 us
    reshape x2, local copies, waits for them, and re-layouts, tile_backward(): pair_tiles[:, :, :model_width].reshape(-1, head_count, head_width)  14.4 us
    ppermute x8, starting transfers between devices, from_behind(): return lax.ppermute(value, axis, pairs)  14.4 us
  transfers between devices with their start and end apart: 9, of which 2 were waited for; matrix products, arithmetic and copies ran while one was open for 17% of the time, Pallas kernels for 0%

commit v1 on v0

--- a/solution.py
+++ b/solution.py
@@ -169,7 +169,7 @@
     local_out = jnp.einsum(
         "pd,pe->de", attended_rows, grad_rows, preferred_element_type=jnp.float32
     )
-    summed_qkv, summed_out = lax.psum((local_qkv, local_out), ("patch", "sample"))
+    summed_qkv, summed_out = lax.psum(lax.psum((local_qkv, local_out), "sample"), "patch")
     factor = float(lax.axis_size("patch") * lax.axis_size("sample") * rows_local) ** (-0.5)
     return (grad_inputs.astype(jnp.bfloat16)[None], summed_qkv * factor, summed_out * factor)
 

time: 487 us -> 590 us (1.21)
  waiting for transfers between devices: 146 us -> 249 us
    psum x1 -> x2, waiting for transfers between devices: 140 us -> 243 us  [the longest x1 156 us: on_device(): lax.psum(lax.psum((local_qkv, local_out), 'sample'), 'patch')]
  transfers between devices with their start and end apart: 9 -> 10, of which waited for: 2 -> 3; matrix products, arithmetic and copies ran while one was open for 17% -> 14% of each run, Pallas kernels for 0% -> 0%
where the time goes in v1:
time: 590 us; the launch traced here: 587 us
  waiting for transfers between devices  249 us (42%)
  local copies, waits for them, and re-layouts  126 us (21%)
  other arithmetic  99.9 us (17%)
  matrix products  83.7 us (14%)
  starting transfers between devices  14.5 us (2%)
  between operations  14.4 us (2%)
    psum x1, waiting for transfers between devices, on_device(): lax.psum(lax.psum((local_qkv, local_out), 'sample'), 'patch')  156 us
    psum x1, waiting for transfers between devices, on_device(): lax.psum((local_qkv, local_out), 'sample')  87 us
    scatter-add x1, other arithmetic, advance(): running.at[flat_slots]  35.9 us
    dot_general x1, matrix products, tile_backward(): jnp.einsum('hqk,qhd->khd', dscore, query_heads, preferred_element_type=jn...  23.7 us
    dot_general x1, matrix products, tile_backward(): jnp.einsum('hqk,khd->qhd', dscore, key_heads, preferred_element_type=jnp....  22.8 us
    concatenate x2, local copies, waits for them, and re-layouts, tile_backward(): return (attended, dquery, jnp.concatenate([dkey, dvalue], -1))  20.5 us
    reshape x2, local copies, waits for them, and re-layouts, tile_backward(): pair_tiles[:, :, model_width:].reshape(-1, head_count, head_width)  14.5 us
    reshape x2, local copies, waits for them, and re-layouts, tile_backward(): pair_tiles[:, :, :model_width].reshape(-1, head_count, head_width)  14.4 us
  transfers between devices with their start and end apart: 10, of which 3 were waited for; matrix products, arithmetic and copies ran while one was open for 14% of the time, Pallas kernels for 0%

profile of v1, /device:TPU:0, one launch (start us, length us, event | category | flops | bytes accessed | tf_op | source)
XLA Modules:
  0.0 587.4 jit_solution(11026103215495468854)
XLA Ops:
  14.5 1.9 broadcast_select_fusion.1
  16.4 5.1 collective-permute-start.3
  22.9 2.0 broadcast_select_fusion.2
  28.2 2.0 broadcast_select_fusion.3
  36.9 2.5 convolution_convert_fusion.1
  41.3 2.0 reshape.469
  43.3 2.1 copy.88
  45.4 2.0 reshape.470
  47.3 2.0 copy.90
  50.4 6.0 %collective-permute-done = bf16[2,128,1024]{2,1,0:T(8,128)(2,1)} collective-permute-done((bf16[2,128,1024]{2,1,0:T(8,128)(2,1)}, bf16[2,128,1024]{2,1,0:T(8,128)(2,1)}, u32[]{:S(2)}, u32[]{:S(2)}) %collective-permute-start) | collective-permute-done | bytes 524320 | tf_op jit(solution)/shard_map/ppermute | solution.py:19
  63.9 7.0 %gather_fusion = bf16[32,128,1024]{2,1,0:T(8,128)(2,1)} fusion(bf16[12,128,1024]{2,1,0:T(8,128)(2,1)} %constant_dynamic-update-slice_fusion, s32[1024]{0:T(1024)S(1)} %pad_clamp_fusion), kind=kCustom, calls=%fused_computation.4 | custom fusion | bytes 16777344 | tf_op jit(solution)/shard_map/while/body/eval_jaxpr/jit(_take)/gather | solution.py:130
  70.9 7.5 %broadcast_select_fusion = bf16[4,8,128,1024]{3,2,1,0:T(8,128)(2,1)} fusion(bf16[4,8,128,1024]{3,2,1,0:T(8,128)(2,1)} %bitcast.111, pred[4,8]{1,0:T(4,128)(4,1)S(1)} %get-tuple-element.55), kind=kLoop, calls=%fused_computation.18 | loop fusion | flops 4194304 | bytes 16777248 | tf_op jit(solution)/shard_map/while/body/eval_jaxpr/jit(_take)/select_n | solution.py:130
  78.4 5.9 %fusion.74 = (bf16[4,8,128,512]{3,2,1,0:T(8,128)(2,1)}, bf16[4,8,128,512]{3,2,1,0:T(8,128)(2,1)}) fusion(bf16[4,8,128,1024]{3,2,1,0:T(8,128)(2,1)} %broadcast_select_fusion), kind=kLoop, calls=%fused_computation.171 | loop fusion | bytes 16777216 | tf_op jit(solution)/shard_map/while/body/eval_jaxpr/vmap()/slice | solution.py:28
  84.2 6.9 %reshape.576 = bf16[4,1024,4,128]{3,2,1,0:T(4,128)(2,1)} reshape(bf16[4,8,128,512]{3,2,1,0:T(8,128)(2,1)} %get-tuple-element.58) | data formatting | bytes 8388608 | tf_op jit(solution)/shard_map/while/body/eval_jaxpr/vmap()/reshape | solution.py:27
  91.2 7.5 %copy.96 = bf16[4,1024,4,128]{1,3,2,0:T(8,128)(2,1)} copy(bf16[4,1024,4,128]{3,2,1,0:T(4,128)(2,1)} %reshape.576) | data formatting | bytes 8388608 | tf_op jit(solution)/shard_map/while/body/eval_jaxpr/vmap()/reshape | solution.py:27
  98.7 6.9 %reshape.577 = bf16[4,1024,4,128]{3,2,1,0:T(4,128)(2,1)} reshape(bf16[4,8,128,512]{3,2,1,0:T(8,128)(2,1)} %get-tuple-element.57) | data formatting | bytes 8388608 | tf_op jit(solution)/shard_map/while/body/eval_jaxpr/vmap()/reshape | solution.py:28
  105.6 7.6 %copy.95 = bf16[4,1024,4,128]{1,3,2,0:T(8,128)(2,1)} copy(bf16[4,1024,4,128]{3,2,1,0:T(4,128)(2,1)} %reshape.577) | data formatting | bytes 8388608 | tf_op jit(solution)/shard_map/while/body/eval_jaxpr/vmap()/reshape | solution.py:28
  113.2 6.8 %fusion.77 = f32[4,4,128,1024]{3,2,1,0:T(8,128)} fusion(bf16[4,128,4,128]{1,3,2,0:T(8,128)(2,1)S(1)} %copy-done.3, bf16[4,1024,4,128]{1,3,2,0:T(8,128)(2,1)} %copy.95), kind=kOutput, calls=%fused_computation.174 | convolution fusion | flops 536870912 | bytes 13107200 | tf_op jit(solution)/shard_map/while/body/eval_jaxpr/vmap(qhd,khd->hqk)/dot_general | solution.py:45
  120.0 8.5 %fusion.76 = (f32[4,4,128]{2,1,0:T(4,128)S(1)}, f32[4,4,128,1024]{3,2,1,0:T(8,128)}) fusion(pred[4,1024]{1,0:T(4,128)(4,1)S(1)} %bitcast.123, bf16[4,128,4,128]{1,3,2,0:T(8,128)(2,1)S(1)} %copy-done.7, bf16[4,1024,4,128]{1,3,2,0:T(8,128)(2,1)} %copy.96), kind=kOutput, calls=%fused_computation.173 | convolution fusion | flops 545260544 | bytes 13119488 | tf_op jit(solution)/shard_map/while/body/eval_jaxpr/vmap()/sub | solution.py:38
  128.5 6.9 %fusion.30 = bf16[4,128,4,128]{1,3,2,0:T(8,128)(2,1)} fusion(bf16[4,1024,4,128]{1,3,2,0:T(8,128)(2,1)} %copy.95, f32[4,4,128,1024]{3,2,1,0:T(8,128)} %get-tuple-element.69, f32[4,4,128]{2,1,0:T(4,128)S(1)} %get-tuple-element.68), kind=kOutput, calls=%fused_computation.42 | convolution fusion | flops 541327360 | bytes 13115392 | tf_op jit(solution)/shard_map/while/body/eval_jaxpr/vmap(hqk,khd->qhd)/dot_general | solution.py:41
  135.5 4.0 convolution_bitcast_fusion
  139.6 23.7 %fusion.15 = f32[4,1024,4,128]{1,3,2,0:T(8,128)} fusion(bf16[4,128,4,128]{1,3,2,0:T(8,128)(2,1)S(1)} %copy-done.7, f32[4,4,128,1024]{3,2,1,0:T(8,128)} %fusion.77, f32[4,4,128,1024]{3,2,1,0:T(8,128)} %get-tuple-element.69, f32[4,4,128]{2,1,0:T(4,128)S(1)} %get-tuple-element.68), kind=kOutput, calls=%fused_computation.26 | convolution fusion | flops 551554048 | bytes 25698304 | tf_op jit(solution)/shard_map/while/body/eval_jaxpr/vmap(hqk,qhd->khd)/dot_general | solution.py:51
  163.3 9.9 %copy.89 = f32[4,1024,4,128]{3,2,1,0:T(4,128)} copy(f32[4,1024,4,128]{1,3,2,0:T(8,128)} %fusion.15) | data formatting | bytes 16777216 | tf_op jit(solution)/shard_map/while/body/eval_jaxpr/vmap(hqk,qhd->khd)/transpose | solution.py:51
  173.2 10.3 %concatenate.21 = f32[32,128,512]{2,1,0:T(8,128)} reshape(f32[4,1024,4,128]{3,2,1,0:T(4,128)} %copy.89) | data formatting | bytes 16777216 | tf_op jit(solution)/shard_map/while/body/eval_jaxpr/vmap()/concatenate | solution.py:57
  183.4 9.9 %copy.91 = f32[4,1024,4,128]{3,2,1,0:T(4,128)} copy(f32[4,1024,4,128]{1,3,2,0:T(8,128)} %convolution_bitcast_fusion) | data formatting | bytes 16777216 | tf_op jit(solution)/shard_map/while/body/eval_jaxpr/vmap(hqk,qhd->khd)/transpose | solution.py:52
  193.3 10.3 %concatenate.22 = f32[32,128,512]{2,1,0:T(8,128)} reshape(f32[4,1024,4,128]{3,2,1,0:T(4,128)} %copy.91) | data formatting | bytes 16777216 | tf_op jit(solution)/shard_map/while/body/eval_jaxpr/vmap()/concatenate | solution.py:57
  203.6 11.7 %pad_maximum_fusion = f32[32,128,1024]{2,1,0:T(8,128)} fusion(f32[32,128,512]{2,1,0:T(8,128)} %concatenate.22, f32[32,128,512]{2,1,0:T(8,128)} %concatenate.21), kind=kLoop, calls=%fused_computation.12 | loop fusion | flops 4194304 | bytes 33554432 | tf_op jit(solution)/shard_map/while/body/eval_jaxpr/vmap()/concatenate | solution.py:57
  215.3 3.4 broadcast_in_dim.161
  218.7 35.9 %scatter_fusion = f32[12,128,1024]{2,1,0:T(8,128)} fusion(f32[12,128,1024]{2,1,0:T(8,128)} %broadcast_in_dim.161, s32[32]{0:T(128)S(1)} %fusion.61, f32[32,128,1024]{2,1,0:T(8,128)} %pad_maximum_fusion), kind=kCustom, calls=%fused_computation.5 | custom fusion | flops 4194304 | bytes 50331776 | tf_op jit(solution)/shard_map/while/body/eval_jaxpr/scatter-add | solution.py:134
  254.6 4.9 convert.25
  259.6 3.2 slice.56
  263.9 2.9 fusion.75
  266.8 3.3 collective-permute-start.4
  273.1 22.8 %fusion.33 = bf16[4,128,4,128]{1,3,2,0:T(8,128)(2,1)S(1)} fusion(bf16[4,1024,4,128]{1,3,2,0:T(8,128)(2,1)} %copy.96, f32[4,4,128,1024]{3,2,1,0:T(8,128)} %fusion.77, f32[4,4,128,1024]{3,2,1,0:T(8,128)} %get-tuple-element.69, f32[4,4,128]{2,1,0:T(4,128)S(1)} %get-tuple-element.68), kind=kOutput, calls=%fused_computation.43 | convolution fusion | flops 551816192 | bytes 21504000 | tf_op jit(solution)/shard_map/while/body/eval_jaxpr/vmap(hqk,khd->qhd)/dot_general | solution.py:48
  298.2 2.5 fusion.45
  300.7 2.1 convert_element_type.189
  302.8 3.4 scatter_fusion.1
  306.2 2.1 convert_element_type.190
  308.3 3.4 scatter_fusion.2
  311.8 2.1 convert_element_type.191
  313.9 3.4 scatter_fusion.3
  317.3 2.1 convert_element_type.192
  319.4 3.4 scatter_fusion.4
  325.5 2.7 fusion.42
  328.3 87.0 %all-reduce.7.cloned.1.call-done = (f32[512,1536]{1,0:T(8,128)}, f32[512,512]{1,0:T(8,128)}) async-done(((f32[512,1536]{1,0:T(8,128)}, f32[512,512]{1,0:T(8,128)}), (f32[512,1536]{1,0:T(8,128)}, f32[512,512]{1,0:T(8,128)})) %all-reduce.7.cloned.1.call-update) | async-done | bytes 4194320 | tf_op jit(solution)/shard_map/psum | solution.py:172
  416.3 2.3 fusion.36
  419.9 155.7 %all-reduce.5.cloned.1.call-done = (f32[512,1536]{1,0:T(8,128)}, f32[512,512]{1,0:T(8,128)}) async-done(((f32[512,1536]{1,0:T(8,128)}, f32[512,512]{1,0:T(8,128)}), (f32[512,1536]{1,0:T(8,128)}, f32[512,512]{1,0:T(8,128)})) %all-reduce.5.cloned.1.call-update) | async-done | bytes 4194320 | tf_op jit(solution)/shard_map/psum | solution.py:172
  575.6 3.9 broadcast_multiply_fusion
  (129 shorter events, 41.5 us)
Async XLA Ops:
  7.2 3.7 copy-start
  7.2 408.1 %all-reduce.7.cloned.1.call-start = ((), (), s32[]{:S(2)}) async-start(), calls=%async_computation.1 | async-start | bytes 8388608 | tf_op jit(solution)/shard_map/psum | solution.py:172
  11.9 1.1 copy-start.5
  13.1 23.5 %copy-start.9 = (s32[32,8]{0,1:T(8,128)S(1)}, s32[32,8]{0,1:T(8,128)}, u32[]{:S(2)}) copy-start(s32[32,8]{0,1:T(8,128)} %param.13) | copy-start | bytes 3076
  16.4 45.6 %collective-permute-start.3 = (bf16[2,128,1024]{2,1,0:T(8,128)(2,1)}, bf16[2,128,1024]{2,1,0:T(8,128)(2,1)}, u32[]{:S(2)}, u32[]{:S(2)}) collective-permute-start(bf16[2,128,1024]{2,1,0:T(8,128)(2,1)} %broadcast_select_fusion.1), channel_id=1, source_target_pairs={{0,24},{4,28},{8,0},{12,4},{16,8},{20,12},{24,16},{28,20},{1,25},{... | collective-permute-start | bytes 1572872 | tf_op jit(solution)/shard_map/ppermute | solution.py:19
  24.9 35.3 %collective-permute-start.2 = (bf16[2,128,1024]{2,1,0:T(8,128)(2,1)}, bf16[2,128,1024]{2,1,0:T(8,128)(2,1)}, u32[]{:S(2)}, u32[]{:S(2)}) collective-permute-start(bf16[2,128,1024]{2,1,0:T(8,128)(2,1)} %broadcast_select_fusion.2), channel_id=1, source_target_pairs={{0,28},{4,0},{8,4},{12,8},{16,12},{20,16},{24,20},{28,24},{1,29},{... | collective-permute-start | bytes 1572872 | tf_op jit(solution)/shard_map/ppermute | solution.py:19
  30.2 28.1 %collective-permute-start.1 = (bf16[2,128,1024]{2,1,0:T(8,128)(2,1)}, bf16[2,128,1024]{2,1,0:T(8,128)(2,1)}, u32[]{:S(2)}, u32[]{:S(2)}) collective-permute-start(bf16[2,128,1024]{2,1,0:T(8,128)(2,1)} %broadcast_select_fusion.3), channel_id=1, source_target_pairs={{0,4},{4,8},{8,12},{12,16},{16,20},{20,24},{24,28},{28,0},{1,5},{5... | collective-permute-start | bytes 1572872 | tf_op jit(solution)/shard_map/ppermute | solution.py:19
  34.2 22.3 %collective-permute-start = (bf16[2,128,1024]{2,1,0:T(8,128)(2,1)}, bf16[2,128,1024]{2,1,0:T(8,128)(2,1)}, u32[]{:S(2)}, u32[]{:S(2)}) collective-permute-start(bf16[2,128,1024]{2,1,0:T(8,128)(2,1)} %broadcast_select_fusion.4), channel_id=1, source_target_pairs={{0,8},{4,12},{8,16},{12,20},{16,24},{20,28},{24,0},{28,4},{1,9},{5... | collective-permute-start | bytes 1572872 | tf_op jit(solution)/shard_map/ppermute | solution.py:19
  105.6 7.6 %copy-start.3 = (bf16[4,128,4,128]{1,3,2,0:T(8,128)(2,1)S(1)}, bf16[4,128,4,128]{1,3,2,0:T(8,128)(2,1)}, u32[]{:S(2)}) copy-start(bf16[4,128,4,128]{1,3,2,0:T(8,128)(2,1)} %copy.90) | copy-start | bytes 1572868
  113.2 6.8 %copy-start.7 = (bf16[4,128,4,128]{1,3,2,0:T(8,128)(2,1)S(1)}, bf16[4,128,4,128]{1,3,2,0:T(8,128)(2,1)}, u32[]{:S(2)}) copy-start(bf16[4,128,4,128]{1,3,2,0:T(8,128)(2,1)} %copy.88) | copy-start | bytes 1572868
  128.5 7.0 %copy-start.10 = (f32[4,4,128,1024]{3,2,1,0:T(8,128)S(1)}, f32[4,4,128,1024]{3,2,1,0:T(8,128)}, u32[]{:S(2)}) copy-start(f32[4,4,128,1024]{3,2,1,0:T(8,128)} %get-tuple-element.69) | copy-start | bytes 25165828
  259.6 3.2 copy-start.8
  266.8 33.9 %collective-permute-start.4 = (bf16[2,128,1024]{2,1,0:T(8,128)(2,1)}, bf16[2,128,1024]{2,1,0:T(8,128)(2,1)}, u32[]{:S(2)}, u32[]{:S(2)}) collective-permute-start(bf16[2,128,1024]{2,1,0:T(8,128)(2,1)} %get-tuple-element.62), channel_id=1, source_target_pairs={{0,24},{4,28},{8,0},{12,4},{16,8},{20,12},{24,16},{28,20},{1,25},{... | collective-permute-start | bytes 1572872 | tf_op jit(solution)/shard_map/ppermute | solution.py:19
  270.1 36.1 %collective-permute-start.5 = (bf16[2,128,1024]{2,1,0:T(8,128)(2,1)}, bf16[2,128,1024]{2,1,0:T(8,128)(2,1)}, u32[]{:S(2)}, u32[]{:S(2)}) collective-permute-start(bf16[2,128,1024]{2,1,0:T(8,128)(2,1)} %get-tuple-element.61), channel_id=1, source_target_pairs={{0,28},{4,0},{8,4},{12,8},{16,12},{20,16},{24,20},{28,24},{1,29},{... | collective-permute-start | bytes 1572872 | tf_op jit(solution)/shard_map/ppermute | solution.py:19
  271.6 40.1 %collective-permute-start.6 = (bf16[2,128,1024]{2,1,0:T(8,128)(2,1)}, bf16[2,128,1024]{2,1,0:T(8,128)(2,1)}, u32[]{:S(2)}, u32[]{:S(2)}) collective-permute-start(bf16[2,128,1024]{2,1,0:T(8,128)(2,1)} %get-tuple-element.60), channel_id=1, source_target_pairs={{0,4},{4,8},{8,12},{12,16},{16,20},{20,24},{24,28},{28,0},{1,5},{5... | collective-permute-start | bytes 1572872 | tf_op jit(solution)/shard_map/ppermute | solution.py:19
  272.1 26.1 %copy-start.1 = (bf16[1,512,512]{2,1,0:T(8,128)(2,1)S(1)}, bf16[1,512,512]{2,1,0:T(8,128)(2,1)}, u32[]{:S(2)}) copy-start(bf16[1,512,512]{2,1,0:T(8,128)(2,1)} %param.9) | copy-start | bytes 1572868
  272.1 45.2 %collective-permute-start.7 = (bf16[2,128,1024]{2,1,0:T(8,128)(2,1)}, bf16[2,128,1024]{2,1,0:T(8,128)(2,1)}, u32[]{:S(2)}, u32[]{:S(2)}) collective-permute-start(bf16[2,128,1024]{2,1,0:T(8,128)(2,1)} %get-tuple-element.59), channel_id=1, source_target_pairs={{0,8},{4,12},{8,16},{12,20},{16,24},{20,28},{24,0},{28,4},{1,9},{5... | collective-permute-start | bytes 1572872 | tf_op jit(solution)/shard_map/ppermute | solution.py:19
  324.6 1.0 copy-start.2
  328.2 247.4 %all-reduce.5.cloned.1.call-start = ((), (), s32[]{:S(2)}) async-start(), calls=%async_computation | async-start | bytes 8388608 | tf_op jit(solution)/shard_map/psum | solution.py:172
  416.3 2.3 copy-start.4
  575.6 3.9 copy-start.6
Sparse Core Ops, SparseCore 0:
  328.3 86.9 all-reduce.6
  419.0 156.5 all-reduce.4
